TPU v7x, 512 devices: a whole 4x8x8 slice. The times are simulated.
512 devices in a mesh: tmpl: 8 (over x, y_hi), freq: 64 (over z, y_lo, core).
Axes of the slice: x: 4, y: 8 (y_hi: 2, y_lo: 4; y = y_hi * 4 + y_lo), z: 8, core: 2. Of those that a mesh axis runs over, the one named last changes fastest.
Arguments:
- strain: float32 [512, 512], P('freq'), may hold values from -6 to 6
- inv_asd: float32 [512, 512], P('freq'), may hold values from 0.25 to 4
- spectra: bfloat16 [512, 64, 2, 512], P('freq', 'tmpl'), may hold values from -6 to 6
- cutoff: int32 [64], P('tmpl'), may hold values from 64 to 256
Outputs:
- filter_series: float32 [64, 2, 512, 512], P('tmpl', None, 'freq')
- peak_power: float32 [512, 512], P('freq')
All inputs are finite; a program needn't handle non-finite values.
Results may differ from a plain program's by a relative error of at most 0.0051.
Values may be sent and summed in bfloat16 or wider, within the bound.
A program may use at most 64 MiB of HBM per device.

v0:
```python
import math

import jax
import jax.numpy as jnp
from jax import lax
from jax.sharding import PartitionSpec as P


def angle_table(left, right, modulus):
    product = left[:, None] * right[None, :] % modulus
    return 2.0 * math.pi / modulus * product.astype(jnp.float32)


def exact_dot(left, right):
    return jnp.dot(left, right, precision=lax.Precision.HIGHEST, preferred_element_type=jnp.float32)


def inverse_first(product, section_table, twist_cos, twist_sin):
    turned = jnp.einsum(
        "ktcj,cjdm->kmtd", product, section_table, preferred_element_type=jnp.float32
    )
    real_part = turned[..., 0]
    imag_part = turned[..., 1]
    rotated = jnp.stack(
        [
            real_part * twist_cos[:, :, None] - imag_part * twist_sin[:, :, None],
            real_part * twist_sin[:, :, None] + imag_part * twist_cos[:, :, None],
        ],
        -1,
    ).astype(jnp.bfloat16)
    return rotated.reshape(rotated.shape[0], -1)


def inverse_last(received, templ_count, last_table, total_size):
    side_size = received.shape[0]
    arranged = received.reshape(side_size, -1, templ_count, 2)
    return jnp.einsum(
        "kmtc,kcdn->tdmn", arranged, last_table, preferred_element_type=jnp.float32
    ) * (1.0 / total_size)


def local(strain, inv_asd, spectra, cutoff):
    row_count = strain.shape[0]
    side_size = strain.shape[1]
    total_size = side_size * side_size
    templ_count = spectra.shape[1]
    positions = jnp.arange(side_size, dtype=jnp.int32)
    local_rows = lax.axis_index("freq") * row_count + jnp.arange(row_count, dtype=jnp.int32)
    full_angle = angle_table(positions, positions, side_size)
    cosines = jnp.cos(full_angle)
    sine_part = jnp.sin(full_angle)
    row_angle = angle_table(local_rows, positions, total_size)
    row_cos = jnp.cos(row_angle)
    row_sin = jnp.sin(row_angle)
    columns = lax.all_to_all(strain, "freq", split_axis=1, concat_axis=0, tiled=True)
    first_real = exact_dot(cosines, columns)
    first_imag = -exact_dot(sine_part, columns)
    twist_angle = angle_table(positions, local_rows, total_size)
    twist_cos = jnp.cos(twist_angle)
    twist_sin = jnp.sin(twist_angle)
    turned = jnp.stack(
        [
            first_real * twist_cos + first_imag * twist_sin,
            first_imag * twist_cos - first_real * twist_sin,
        ],
        1,
    )
    returned = lax.all_to_all(turned, "freq", split_axis=0, concat_axis=2, tiled=True)
    mid_real = returned[:, 0]
    mid_imag = returned[:, 1]
    white_real = (exact_dot(mid_real, cosines) + exact_dot(mid_imag, sine_part)) * inv_asd
    white_imag = (exact_dot(mid_imag, cosines) - exact_dot(mid_real, sine_part)) * inv_asd
    band_mask = (positions[None, :] < cutoff[:, None]).astype(jnp.float32)[None]
    spec_real = spectra[:, :, 0].astype(jnp.float32)
    spec_imag = spectra[:, :, 1].astype(jnp.float32)
    prod_real = (white_real[:, None] * spec_real + white_imag[:, None] * spec_imag) * band_mask
    prod_imag = (white_imag[:, None] * spec_real - white_real[:, None] * spec_imag) * band_mask
    product = jnp.stack([prod_real, prod_imag], 2).astype(jnp.bfloat16)
    base_table = jnp.stack(
        [jnp.stack([cosines, sine_part]), jnp.stack([-sine_part, cosines])]
    ).astype(jnp.bfloat16)
    section_table = jnp.transpose(base_table, (0, 2, 1, 3))
    last_table = jnp.transpose(base_table, (2, 0, 1, 3))
    outgoing = inverse_first(product, section_table, row_cos, row_sin)
    received = lax.all_to_all(outgoing, "freq", split_axis=1, concat_axis=0, tiled=True)
    filter_series = inverse_last(received, templ_count, last_table, total_size)
    power_sum = filter_series[:, 0] ** 2 + filter_series[:, 1] ** 2
    peak_power = lax.pmax(jnp.max(power_sum, axis=0), "tmpl")
    return (filter_series, peak_power)


def solution(mesh):
    in_specs = (P("freq", None), P("freq", None), P("freq", "tmpl", None, None), P("tmpl"))
    out_specs = (P("tmpl", None, "freq", None), P("freq", None))
    return jax.shard_map(local, mesh=mesh, in_specs=in_specs, out_specs=out_specs, check_vma=False)
```

profile of v0, /device:TPU:8, one launch (start us, length us, event | category | flops | bytes accessed | tf_op | source)
XLA Modules:
  0.0 155.4 jit_solution(10834761956163666656)
XLA Ops:
  0.6 0.9 all_to_all.37
  1.6 0.9 copy.20
  2.4 14.4 %all-to-all-start = ((f32[8,64,8]{2,0,1:T(8,128)}), f32[8,64,8]{2,0,1:T(8,128)S(1)}, u32[]{:S(2)}, u32[]{:S(2)}) async-start(f32[8,64,8]{2,0,1:T(8,128)} %copy.20), calls=%async_computation | async-start | bytes 524288 | tf_op jit(solution)/shard_map/all_to_all | solution.py:55
  16.8 4.3 %negate_convert_fusion = (bf16[1,512,512]{2,1,0:T(8,128)(2,1)S(1)}, bf16[1,512,512]{2,1,0:T(8,128)(2,1)S(1)}) fusion(), kind=kLoop, calls=%fused_computation.30 | loop fusion | flops 4456448 | bytes 1048576 | tf_op jit(solution)/shard_map/convert.7
  21.4 0.2 fusion.100
  21.7 4.0 %fusion.42 = bf16[1,512,512]{2,1,0:T(8,128)(2,1)S(1)} fusion(), kind=kLoop, calls=%fused_computation.43 | loop fusion | flops 3932160 | bytes 524288 | tf_op jit(solution)/shard_map/convert.11
  25.6 3.9 %all-to-all-done = f32[8,64,8]{2,0,1:T(8,128)S(1)} async-done(((f32[8,64,8]{2,0,1:T(8,128)}), f32[8,64,8]{2,0,1:T(8,128)S(1)}, u32[]{:S(2)}, u32[]{:S(2)}) %all-to-all-start) | async-done | bytes 16416 | tf_op jit(solution)/shard_map/all_to_all | solution.py:55
  29.5 4.9 %convolution_negate_fusion = f32[512,8]{0,1:T(8,128)S(1)} fusion(f32[8,64,8]{2,0,1:T(8,128)S(1)} %all-to-all-done), kind=kOutput, calls=%fused_computation.19 | convolution fusion | flops 28839936 | bytes 32768 | tf_op jit(solution)/shard_map/dot_general | solution.py:15
  34.4 4.8 %add_bitcast_fusion = (f32[512,1,8]{0,2,1:T(8,128)S(1)}, f32[512,1,8]{0,2,1:T(8,128)S(1)}) fusion(f32[512,8]{0,1:T(8,128)S(1)} %convolution_negate_fusion, s32[8]{0:T(128)S(1)} %iota_add_fusion, f32[8,64,8]{2,0,1:T(8,128)S(1)} %all-to-all-done), kind=kOutput, calls=%fused_computation.87 | convolution fusion | flops 28917760 | bytes 65568 | tf_op jit(solution)/shard_map/dot_general | solution.py:15
  39.3 0.2 copy.22
  39.5 1.4 reshape.188
  40.9 6.8 %all-to-all-start.1 = ((f32[64,1,128]{2,1,0:T(1,128)}), f32[64,1,128]{2,1,0:T(1,128)S(1)}, u32[]{:S(2)}, u32[]{:S(2)}) async-start(f32[64,1,128]{2,1,0:T(1,128)} %reshape.188), calls=%async_computation.1 | async-start | bytes 65536 | tf_op jit(solution)/shard_map/all_to_all | solution.py:68
  47.7 1.2 maximum_bitcast_fusion
  48.8 7.7 %all-to-all-done.1 = f32[64,1,128]{2,1,0:T(1,128)S(1)} async-done(((f32[64,1,128]{2,1,0:T(1,128)}), f32[64,1,128]{2,1,0:T(1,128)S(1)}, u32[]{:S(2)}, u32[]{:S(2)}) %all-to-all-start.1) | async-done | bytes 32800 | tf_op jit(solution)/shard_map/all_to_all | solution.py:68
  56.5 0.5 broadcast.265
  57.0 0.7 reduce.1
  57.7 0.8 reshape.189
  58.6 0.2 copy.50
  58.7 0.3 all_to_all.44
  59.0 4.5 %fusion.32 = f32[8,512]{1,0:T(8,128)S(1)} fusion(f32[8,2,512]{2,0,1:T(8,128)S(1)} %all_to_all.44), kind=kOutput, calls=%fused_computation.39 | convolution fusion | flops 28835840 | bytes 32768 | tf_op jit(solution)/shard_map/dot_general | solution.py:15
  63.5 4.5 %fusion.34 = f32[8,512]{1,0:T(8,128)S(1)} fusion(f32[8,2,512]{2,0,1:T(8,128)S(1)} %all_to_all.44), kind=kOutput, calls=%fused_computation.40 | convolution fusion | flops 28835840 | bytes 32768 | tf_op jit(solution)/shard_map/dot_general | solution.py:15
  68.1 4.6 %fusion.16 = f32[8,512]{1,0:T(8,128)S(1)} fusion(f32[8,512]{1,0:T(8,128)S(1)} %copy-done.3, f32[8,512]{1,0:T(8,128)S(1)} %fusion.32, f32[8,2,512]{2,0,1:T(8,128)S(1)} %all_to_all.44), kind=kOutput, calls=%fused_computation.16 | convolution fusion | flops 28844032 | bytes 65536 | tf_op jit(solution)/shard_map/dot_general | solution.py:15
  72.7 4.6 %fusion.17 = f32[8,512]{1,0:T(8,128)S(1)} fusion(f32[8,512]{1,0:T(8,128)S(1)} %copy-done.3, f32[8,512]{1,0:T(8,128)S(1)} %fusion.34, f32[8,2,512]{2,0,1:T(8,128)S(1)} %all_to_all.44), kind=kOutput, calls=%fused_computation.18 | convolution fusion | flops 28844032 | bytes 65536 | tf_op jit(solution)/shard_map/dot_general | solution.py:15
  77.3 0.5 fusion.13
  77.9 1.7 %copy.27 = bf16[8,512,8,2]{0,3,2,1:T(2,128)(2,1)S(1)} copy(bf16[8,512,8,2]{1,2,0,3:T(8,128)(2,1)S(1)} %pad_maximum_fusion.3) | data formatting | bytes 262144 | tf_op jit(solution)/shard_map/stack | solution.py:24
  79.7 0.8 copy.28
  80.5 14.9 %all_to_all.50 = bf16[8,64,128]{2,0,1:T(8,128)(2,1)S(1)} all-to-all(bf16[8,64,128]{2,0,1:T(8,128)(2,1)S(1)} %copy.28), channel_id=1, replica_groups=mesh['tmpl'=8,'freq'=64] {'freq'}, dimensions={1} | all-to-all | bytes 262144 | tf_op jit(solution)/shard_map/all_to_all | solution.py:85
  95.3 2.9 %copy.29 = bf16[64,8,128]{1,0,2:T(8,128)(2,1)S(1)} copy(bf16[64,8,128]{2,1,0:T(8,128)(2,1)S(1)} %bitcast.85) | data formatting | bytes 262144 | tf_op jit(solution)/shard_map/all_to_all | solution.py:85
  98.3 2.3 %reshape.181 = bf16[512,8,8,2]{0,3,2,1:T(2,128)(2,1)S(1)} reshape(bf16[64,8,128]{1,0,2:T(8,128)(2,1)S(1)} %copy.29) | data formatting | bytes 262144 | tf_op jit(solution)/shard_map/reshape | solution.py:36
  100.6 1.7 %fusion.10 = f32[8,2,8,512]{3,0,2,1:T(8,128)S(1)} fusion(bf16[1,2,512,512]{3,2,0,1:T(8,128)(2,1)} %get-tuple-element.9, bf16[1,2,512,512]{3,2,0,1:T(8,128)(2,1)S(1)} %get-tuple-element.8, bf16[512,8,8,2]{0,3,2,1:T(2,128)(2,1)S(1)} %reshape.181), kind=kOutput, calls=%fused_computation.13 | convolution fusion | flops 138477568 | bytes 2490368 | tf_op jit(solution)/shard_map/kmtc,kcdn->tdmn/dot_general | solution.py:37
  102.3 0.9 copy.31
  103.2 52.2 %pmax.7 = f32[8,512]{1,0:T(8,128)} all-reduce(f32[8,512]{1,0:T(8,128)S(1)} %fusion.52), channel_id=1, replica_groups=mesh['tmpl'=8,'freq'=64] {'tmpl'}, use_global_device_ids=true, to_apply=%region_1.2 | all-reduce | flops 4096 | bytes 32768 | tf_op jit(solution)/shard_map/pmax | solution.py:88
  (16 shorter events, 0.4 us)
Async XLA Ops:
  0.6 20.5 %copy-start.2 = (s32[8]{0:T(128)S(1)}, s32[8]{0:T(128)}, u32[]{:S(2)}) copy-start(s32[8]{0:T(128)} %param.7) | copy-start | bytes 100
  0.6 20.8 %copy-start.1 = (bf16[8,8,2,512]{3,2,1,0:T(2,128)(2,1)S(1)}, bf16[8,8,2,512]{3,2,1,0:T(2,128)(2,1)}, u32[]{:S(2)}) copy-start(bf16[8,8,2,512]{3,2,1,0:T(2,128)(2,1)} %param.6) | copy-start | bytes 393220
  2.4 27.1 %all-to-all-start = ((f32[8,64,8]{2,0,1:T(8,128)}), f32[8,64,8]{2,0,1:T(8,128)S(1)}, u32[]{:S(2)}, u32[]{:S(2)}) async-start(f32[8,64,8]{2,0,1:T(8,128)} %copy.20), calls=%async_computation | async-start | bytes 524288 | tf_op jit(solution)/shard_map/all_to_all | solution.py:55
  40.9 15.6 %all-to-all-start.1 = ((f32[64,1,128]{2,1,0:T(1,128)}), f32[64,1,128]{2,1,0:T(1,128)S(1)}, u32[]{:S(2)}, u32[]{:S(2)}) async-start(f32[64,1,128]{2,1,0:T(1,128)} %reshape.188), calls=%async_computation.1 | async-start | bytes 65536 | tf_op jit(solution)/shard_map/all_to_all | solution.py:68
  63.5 4.6 %copy-start.3 = (f32[8,512]{1,0:T(8,128)S(1)}, f32[8,512]{1,0:T(8,128)}, u32[]{:S(2)}) copy-start(f32[8,512]{1,0:T(8,128)} %param.5) | copy-start | bytes 49156
  72.7 4.7 %copy-start = (bf16[1,2,512,512]{3,2,0,1:T(8,128)(2,1)S(1)}, bf16[1,2,512,512]{3,2,0,1:T(8,128)(2,1)}, u32[]{:S(2)}) copy-start(bf16[1,2,512,512]{3,2,0,1:T(8,128)(2,1)} %get-tuple-element.9) | copy-start | bytes 3145732
where the time goes:
time: 156 us; the launch traced here: 155 us
  blocking collectives  67.1 us (43%)
  matrix products  30.1 us (19%)
  starting transfers between devices  21.1 us (14%)
  local copies, waits for them, and re-layouts  14 us (9%)
  waiting for transfers between devices  11.5 us (7%)
  other arithmetic  10.6 us (7%)
    pmax x1, blocking collectives, local(): peak_power = lax.pmax(jnp.max(power_sum, axis=0), 'tmpl')  52.2 us
    dot_general x6, matrix products, exact_dot(): jnp.dot(left, right, precision=lax.Precision.HIGHEST, preferred_element_t...  28 us
    all_to_all x1, blocking collectives, local(): lax.all_to_all(outgoing, 'freq', split_axis=1, concat_axis=0, tiled=True)  14.9 us
    all_to_all x1, starting transfers between devices, local(): lax.all_to_all(strain, 'freq', split_axis=1, concat_axis=0, tiled=True)  14.4 us
    another operation x4, other arithmetic  8.4 us
    all_to_all x1, waiting for transfers between devices, local(): lax.all_to_all(turned, 'freq', split_axis=0, concat_axis=2, tiled=True)  7.67 us
    all_to_all x1, starting transfers between devices, local(): lax.all_to_all(turned, 'freq', split_axis=0, concat_axis=2, tiled=True)  6.77 us
    all_to_all x1, waiting for transfers between devices, local(): lax.all_to_all(strain, 'freq', split_axis=1, concat_axis=0, tiled=True)  3.86 us
  transfers between devices with their start and end apart: 2, of which 2 were waited for; matrix products, arithmetic and copies ran while one was open for 6% of the time, Pallas kernels for 0%

commit v1 on v0

v1 whole, which is shorter than its diff:
```python
import functools
import math

import jax
import jax.numpy as jnp
import numpy as np
from jax import lax
from jax.experimental import pallas as pl
from jax.experimental.pallas import tpu as pltpu
from jax.sharding import PartitionSpec as P

SIDE = 512
BAND = 256
TOTAL = SIDE * SIDE
NZ = 8
NY = 4
NC = 2
NW = NY * NC
NX = 4
NH = 2
NF = NZ * NW
ROWS = SIDE // NF
TEMPL = 8
PAIRS = 2 * TEMPL
MESH = pl.DeviceIdType.MESH
F32 = jnp.float32
BF16 = jnp.bfloat16


def base_tables():
    index = np.arange(SIDE)
    angle = 2.0 * np.pi / SIDE * (np.outer(index, index) % SIDE)
    cosines = np.cos(angle).astype(np.float32)
    sines = np.sin(angle).astype(np.float32)
    whole = np.concatenate([cosines, sines], 1)
    high = whole.astype(jnp.bfloat16)
    part = np.concatenate([cosines[:, :BAND], sines[:, :BAND]], 1)
    low = (part - part.astype(jnp.bfloat16).astype(np.float32)).astype(jnp.bfloat16)
    return high, low


def iota(shape, axis):
    return lax.broadcasted_iota(jnp.int32, shape, axis)


def dot(left, right):
    return jnp.dot(left, right, preferred_element_type=F32)


def split(value):
    high = value.astype(BF16)
    return high, (value - high.astype(F32)).astype(BF16)


def regroup(values):
    lane = iota((ROWS, 128), 1)
    for bit in range(4):
        low = 1 << bit
        width = ROWS * low
        keep = (lane & width) == 0
        moved = list(values)
        for first in range(PAIRS):
            if first & low:
                continue
            second = first | low
            moved[first] = jnp.where(keep, values[first], pltpu.roll(values[second], width, 1))
            moved[second] = jnp.where(keep, pltpu.roll(values[first], 128 - width, 1), values[second])
        values = moved
    return values


def kernel(
    strain, inv_asd, spectra, cutoff, high_table, low_table, series, peak,
    table, table_low, strain_v, asd_v, spectra_v, cut_s, gathered, partial, partials,
    weights, outgoing, received, best, bests, best_half, other_half,
    load_sem, z_send, z_recv, w_send, w_recv, done_sem, f_send, f_recv, x_send, x_recv, h_send, h_recv,
):
    me_t = lax.axis_index("tmpl")
    me_f = lax.axis_index("freq")
    z_pos = me_f // NW
    w_pos = me_f % NW
    core = me_f % NC
    x_pos = me_t // NH
    half = me_t % NH
    y_full = half * NY + w_pos // NC

    loads = [
        pltpu.make_async_copy(strain, strain_v, load_sem.at[0]),
        pltpu.make_async_copy(spectra.at[:, :, :, pl.ds(0, BAND)], spectra_v, load_sem.at[1]),
        pltpu.make_async_copy(inv_asd.at[:, pl.ds(0, BAND)], asd_v, load_sem.at[2]),
        pltpu.make_async_copy(cutoff, cut_s, load_sem.at[3]),
        pltpu.make_async_copy(high_table, table, load_sem.at[4]),
        pltpu.make_async_copy(low_table, table_low, load_sem.at[5]),
    ]
    for load in loads:
        load.start()

    barrier = pltpu.get_barrier_semaphore()

    def greet(device):
        pl.semaphore_signal(barrier, inc=1, device_id=device, device_id_type=MESH)

    for step in range(1, NZ):
        greet((me_t, (z_pos + step) % NZ * NW + w_pos))
    columns = NH * NY * NC
    for step in range(1, columns):
        place = (y_full * NC + core + step) % columns
        greet((x_pos * NH + place // NW, z_pos * NW + place % NW))
    for step in range(1, NX):
        greet(((x_pos + step) % NX * NH + half, me_f))

    loads[0].wait()
    own = strain_v[...]
    gathered[z_pos] = jnp.concatenate([own[:, :BAND], own[:, BAND:]], 0).astype(BF16)

    pl.semaphore_wait(barrier, NZ - 1 + columns - 1 + NX - 1)

    z_copies = []
    for step in range(1, NZ):
        copy = pltpu.make_async_remote_copy(
            src_ref=gathered.at[z_pos], dst_ref=gathered.at[z_pos], send_sem=z_send, recv_sem=z_recv,
            device_id=(me_t, (z_pos + step) % NZ * NW + w_pos), device_id_type=MESH,
        )
        copy.start()

    row = iota((128, 128), 0)
    col = iota((128, 128), 1)
    freq_row = 64 * z_pos + 8 * (row // 16) + row % 8
    sample_row = 64 * (col // 16) + 8 * w_pos + col % 8
    turns = (freq_row * sample_row + 128 * (row // 8 % 2)) & (SIDE - 1)
    first = jnp.cos(turns.astype(F32) * (2.0 * math.pi / SIDE))
    side = col // 8 % 2
    first = jnp.concatenate([jnp.where(side == 0, first, 0.0), jnp.where(side == 1, first, 0.0)], 0)
    first_high, first_low = split(first)
    twist = (ROWS * me_f + iota((ROWS, SIDE), 0)) * iota((ROWS, SIDE), 1)
    twist = twist.astype(F32) * (2.0 * math.pi / TOTAL)
    twist_cos = jnp.cos(twist)
    twist_sin = jnp.sin(twist)

    loads[1].wait()
    loads[2].wait()
    loads[3].wait()
    wanted = row % 8 * PAIRS + row // 8 % 8 * 2 + row // 64
    order = jnp.where(col == wanted, 1.0, 0.0).astype(BF16)
    sorted_spectra = dot(order, spectra_v[...].reshape(128, BAND))
    scale = asd_v[...]
    lane = iota((ROWS, BAND), 1)
    for templ in range(TEMPL):
        gain = jnp.where(lane < cut_s[templ], scale, 0.0)
        for part in range(2):
            block = slice((part * TEMPL + templ) * ROWS, (part * TEMPL + templ + 1) * ROWS)
            weights[block, :] = sorted_spectra[block, :] * gain

    pltpu.make_async_copy(gathered.at[pl.ds(0, NZ - 1)], gathered.at[pl.ds(0, NZ - 1)], z_recv).wait()
    for step in range(1, NW):
        pl.semaphore_signal(
            done_sem, inc=1, device_id=(me_t, z_pos * NW + (w_pos + step) % NW), device_id_type=MESH
        )
    blocks = gathered[...].reshape(128, BAND)
    shares = dot(first_high, blocks) + dot(first_low, blocks)
    partial[:, :, :BAND] = shares[:128].reshape(NW, 16, BAND).astype(BF16)
    partial[:, :, BAND:] = shares[128:].reshape(NW, 16, BAND).astype(BF16)
    for step in range(NY):
        for to_core in range(NC):
            if step == 2:
                away = 2 if to_core == 0 else 6
            else:
                away = (0, 1, 2, 7)[step]
            place = (y_full + away) % (NH * NY)
            target_core = to_core
            target_w = place % NY * NC + target_core
            if step == 0:
                if to_core == 0:
                    continue
                target_w = w_pos // NC * NC + (1 - core)
            copy = pltpu.make_async_remote_copy(
                src_ref=partial.at[target_w], dst_ref=partials.at[w_pos], send_sem=w_send, recv_sem=w_recv,
                device_id=(x_pos * NH + place // NY, z_pos * NW + target_w), device_id_type=MESH,
            )
            copy.start()
    partials[w_pos] = partial[w_pos]
    pltpu.make_async_copy(partials.at[pl.ds(0, NW - 1)], partials.at[pl.ds(0, NW - 1)], w_recv).wait()
    sums = partials[0].astype(F32)
    for slot in range(1, NW):
        sums = sums + partials[slot].astype(F32)
    sum_real = sums[:ROWS]
    sum_imag = sums[ROWS:]
    turned = jnp.concatenate(
        [sum_real * twist_cos + sum_imag * twist_sin, sum_imag * twist_cos - sum_real * twist_sin], 0
    )
    turned_high, turned_low = split(turned)

    loads[4].wait()
    loads[5].wait()
    both = jnp.concatenate([turned_high, turned_low], 0)
    by_cos = dot(both, table[:, :BAND])
    by_sin = dot(both, table[:, SIDE : SIDE + BAND])
    by_cos = by_cos[:16] + by_cos[16:] + dot(turned_high, table_low[:, :BAND])
    by_sin = by_sin[:16] + by_sin[16:] + dot(turned_high, table_low[:, BAND:])
    spec_real = by_cos[:ROWS] + by_sin[ROWS:]
    spec_imag = by_cos[ROWS:] - by_sin[:ROWS]

    product = []
    for templ in range(TEMPL):
        gain_real = weights[templ * ROWS : (templ + 1) * ROWS, :]
        gain_imag = weights[(TEMPL + templ) * ROWS : (TEMPL + templ + 1) * ROWS, :]
        product.append(spec_real * gain_real + spec_imag * gain_imag)
    for templ in range(TEMPL):
        gain_real = weights[templ * ROWS : (templ + 1) * ROWS, :]
        gain_imag = weights[(TEMPL + templ) * ROWS : (TEMPL + templ + 1) * ROWS, :]
        product.append(spec_imag * gain_real - spec_real * gain_imag)
    product = jnp.concatenate(product, 0).astype(BF16)

    pl.semaphore_wait(done_sem, NW - 1)
    for pair in range(2):
        start = pair * 256
        by_cos = dot(product, table[:BAND, start : start + 256])
        by_sin = dot(product, table[:BAND, SIDE + start : SIDE + start + 256])
        for inner in range(2):
            column = 2 * pair + inner
            here = slice(inner * 128, (inner + 1) * 128)
            cos_here = twist_cos[:, column * 128 : (column + 1) * 128]
            sin_here = twist_sin[:, column * 128 : (column + 1) * 128]
            reals = []
            imags = []
            for templ in range(TEMPL):
                up = slice(templ * ROWS, (templ + 1) * ROWS)
                down = slice((TEMPL + templ) * ROWS, (TEMPL + templ + 1) * ROWS)
                real_part = by_cos[up, here] - by_sin[down, here]
                imag_part = by_sin[up, here] + by_cos[down, here]
                reals.append(real_part * cos_here - imag_part * sin_here)
                imags.append(real_part * sin_here + imag_part * cos_here)
            for slot, tile in enumerate(regroup(reals + imags)):
                outgoing[column * 16 + slot] = tile.astype(BF16)

    def send(step, carry):
        target = (me_f + step) % NF
        pltpu.make_async_remote_copy(
            src_ref=outgoing.at[target], dst_ref=received.at[me_f], send_sem=f_send, recv_sem=f_recv,
            device_id=(me_t, target), device_id_type=MESH,
        ).start()
        return carry

    lax.fori_loop(1, NF, send, 0)
    received[me_f] = outgoing[me_f]
    pltpu.make_async_copy(received.at[pl.ds(0, NF - 1)], received.at[pl.ds(0, NF - 1)], f_recv).wait()

    columns_in = jnp.transpose(received[...].reshape(SIDE, 128))
    for pair in range(2):
        start = pair * 256
        by_cos = dot(columns_in, table[:, start : start + 256]) * (1.0 / TOTAL)
        by_sin = dot(columns_in, table[:, SIDE + start : SIDE + start + 256]) * (1.0 / TOTAL)
        top = None
        for templ in range(TEMPL):
            up = slice(templ * ROWS, (templ + 1) * ROWS)
            down = slice((TEMPL + templ) * ROWS, (TEMPL + templ + 1) * ROWS)
            real_part = by_cos[up] - by_sin[down]
            imag_part = by_sin[up] + by_cos[down]
            series[templ, 0, :, start : start + 256] = real_part
            series[templ, 1, :, start : start + 256] = imag_part
            power = real_part * real_part + imag_part * imag_part
            top = power if top is None else jnp.maximum(top, power)
        best[:, start : start + 256] = top

    for step in range(1, NX):
        pltpu.make_async_remote_copy(
            src_ref=best, dst_ref=bests.at[x_pos], send_sem=x_send, recv_sem=x_recv,
            device_id=((x_pos + step) % NX * NH + half, me_f), device_id_type=MESH,
        ).start()
    bests[x_pos] = best[...]
    pltpu.make_async_copy(bests.at[pl.ds(0, NX - 1)], bests.at[pl.ds(0, NX - 1)], x_recv).wait()
    top = jnp.maximum(jnp.maximum(bests[0], bests[1]), jnp.maximum(bests[2], bests[3]))
    best_half[...] = top
    last = pltpu.make_async_remote_copy(
        src_ref=best_half, dst_ref=other_half, send_sem=h_send, recv_sem=h_recv,
        device_id=(x_pos * NH + 1 - half, me_f), device_id_type=MESH,
    )
    last.start()
    last.wait()
    peak[...] = jnp.maximum(top, other_half[...])

    pltpu.make_async_copy(gathered.at[pl.ds(0, NZ - 1)], gathered.at[pl.ds(0, NZ - 1)], z_send).wait()
    pltpu.make_async_copy(partial.at[pl.ds(0, NW - 1)], partial.at[pl.ds(0, NW - 1)], w_send).wait()
    pltpu.make_async_copy(outgoing.at[pl.ds(0, NF - 1)], outgoing.at[pl.ds(0, NF - 1)], f_send).wait()
    pltpu.make_async_copy(bests.at[pl.ds(0, NX - 1)], bests.at[pl.ds(0, NX - 1)], x_send).wait()


def local(strain, inv_asd, spectra, cutoff):
    high, low = base_tables()
    anywhere = pl.BlockSpec(memory_space=pl.ANY)
    inside = pl.BlockSpec(memory_space=pltpu.VMEM)
    dma = pltpu.SemaphoreType.DMA
    return pl.pallas_call(
        kernel,
        out_shape=(
            jax.ShapeDtypeStruct((TEMPL, 2, ROWS, SIDE), F32),
            jax.ShapeDtypeStruct((ROWS, SIDE), F32),
        ),
        in_specs=[anywhere] * 6,
        out_specs=(inside, inside),
        scratch_shapes=[
            pltpu.VMEM((SIDE, 2 * SIDE), BF16),
            pltpu.VMEM((SIDE, SIDE), BF16),
            pltpu.VMEM((ROWS, SIDE), F32),
            pltpu.VMEM((ROWS, BAND), F32),
            pltpu.VMEM((ROWS, TEMPL, 2, BAND), BF16),
            pltpu.SMEM((TEMPL,), jnp.int32),
            pltpu.VMEM((NZ, 16, BAND), BF16),
            pltpu.VMEM((NW, 16, SIDE), BF16),
            pltpu.VMEM((NW, 16, SIDE), BF16),
            pltpu.VMEM((128, BAND), F32),
            pltpu.VMEM((NF, ROWS, 128), BF16),
            pltpu.VMEM((NF, ROWS, 128), BF16),
            pltpu.VMEM((ROWS, SIDE), F32),
            pltpu.VMEM((NX, ROWS, SIDE), F32),
            pltpu.VMEM((ROWS, SIDE), F32),
            pltpu.VMEM((ROWS, SIDE), F32),
            dma((6,)), dma, dma, dma, dma, pltpu.SemaphoreType.REGULAR, dma, dma, dma, dma, dma, dma,
        ],
        compiler_params=pltpu.CompilerParams(collective_id=0, has_side_effects=True),
    )(strain, inv_asd, spectra, cutoff, jnp.asarray(high), jnp.asarray(low))


def solution(mesh):
    in_specs = (P("freq", None), P("freq", None), P("freq", "tmpl", None, None), P("tmpl"))
    out_specs = (P("tmpl", None, "freq", None), P("freq", None))
    return jax.shard_map(local, mesh=mesh, in_specs=in_specs, out_specs=out_specs, check_vma=False)
```

time: 156 us -> 43.2 us (0.28)
  the two profiles are of different devices: /device:TPU:8 before, /device:TPU:1 now
where the time goes in v1:
time: 43.2 us; the launch traced here: 43 us
  Pallas kernels  40.1 us (93%)
  local copies, waits for them, and re-layouts  2.29 us (5%)
  between operations  0.65 us (2%)
    pallas_call x1, Pallas kernels, local(): pl.pallas_call(kernel, out_shape=(jax.ShapeDtypeStruct((TEMPL, 2, ROWS, S...  40.1 us
    unnamed x4, local copies, waits for them, and re-layouts  2.29 us

profile of v1, /device:TPU:1, one launch (start us, length us, event | category | flops | bytes accessed | tf_op | source)
XLA Modules:
  0.0 43.0 jit_solution(9308134536633113503)
XLA Ops:
  0.6 40.1 %shard_map.77 = (f32[8,2,8,512]{3,2,1,0:T(8,128)}, f32[8,512]{1,0:T(8,128)}) custom-call(f32[8,512]{1,0:T(8,128)} %strain.1, f32[8,512]{1,0:T(8,128)} %inv_asd.1, bf16[8,8,2,512]{3,2,1,0:T(2,128)(2,1)} %spectra.1, s32[8]{0:T(128)} %cutoff.1, bf16[512,1024]{1,0:T(8,128)(2,1)} %constant.4.clone.high_table, bf16[512,512]{1,0:T(8,128)(2,1)} %constant.5.clone.low_table), custom_call_target="tpu_custom_call" | custom-call | tf_op jit(solution)/shard_map/pallas_call | solution.py:293
  40.7 0.0 copy-start
  40.7 1.7 %copy.10 = f32[8,2,8,512]{3,2,1,0:T(8,128)} copy(f32[8,2,8,512]{3,2,1,0:T(8,128)} %get-tuple-element.4) | data formatting | bytes 524288
  42.4 0.0 copy-done
  42.4 0.6 %copy.11 = f32[8,512]{1,0:T(8,128)} copy(f32[8,512]{1,0:T(8,128)S(1)} %copy-done) | data formatting | bytes 32768
Async XLA Ops:
  40.7 1.7 %copy-start = (f32[8,512]{1,0:T(8,128)S(1)}, f32[8,512]{1,0:T(8,128)}, u32[]{:S(2)}) copy-start(f32[8,512]{1,0:T(8,128)} %get-tuple-element.5) | copy-start | bytes 49156

commit v2 on v1

--- a/solution.py
+++ b/solution.py
@@ -22,6 +22,7 @@
 ROWS = SIDE // NF
 TEMPL = 8
 PAIRS = 2 * TEMPL
+FAR_FIRST = (4, 3, 5, 2, 6, 1, 7)
 MESH = pl.DeviceIdType.MESH
 F32 = jnp.float32
 BF16 = jnp.bfloat16
@@ -72,8 +73,8 @@
 def kernel(
     strain, inv_asd, spectra, cutoff, high_table, low_table, series, peak,
     table, table_low, strain_v, asd_v, spectra_v, cut_s, gathered, partial, partials,
-    weights, outgoing, received, best, bests, best_half, other_half,
-    load_sem, z_send, z_recv, w_send, w_recv, done_sem, f_send, f_recv, x_send, x_recv, h_send, h_recv,
+    weights, outgoing, received, bests,
+    load_sem, z_send, z_recv, w_send, w_recv, done_sem, ready_sem, f_send, f_recv, t_send, t_recv,
 ):
     me_t = lax.axis_index("tmpl")
     me_f = lax.axis_index("freq")
@@ -100,23 +101,23 @@
     def greet(device):
         pl.semaphore_signal(barrier, inc=1, device_id=device, device_id_type=MESH)
 
-    for step in range(1, NZ):
+    for step in FAR_FIRST:
         greet((me_t, (z_pos + step) % NZ * NW + w_pos))
-    columns = NH * NY * NC
-    for step in range(1, columns):
-        place = (y_full * NC + core + step) % columns
-        greet((x_pos * NH + place // NW, z_pos * NW + place % NW))
-    for step in range(1, NX):
+    for away in (3, 5, 2, 6, 1, 7):
+        place = (y_full + away) % (NH * NY)
+        for to_core in range(NC):
+            greet((x_pos * NH + place // NY, z_pos * NW + place % NY * NC + to_core))
+    greet((me_t, me_f + 1 - 2 * core))
+    for step in (2, 1, 3):
         greet(((x_pos + step) % NX * NH + half, me_f))
 
     loads[0].wait()
     own = strain_v[...]
     gathered[z_pos] = jnp.concatenate([own[:, :BAND], own[:, BAND:]], 0).astype(BF16)
 
-    pl.semaphore_wait(barrier, NZ - 1 + columns - 1 + NX - 1)
-
-    z_copies = []
-    for step in range(1, NZ):
+    pl.semaphore_wait(barrier, NZ - 1 + (NH * NY - 2) * NC + 1 + NX - 1)
+
+    for step in FAR_FIRST:
         copy = pltpu.make_async_remote_copy(
             src_ref=gathered.at[z_pos], dst_ref=gathered.at[z_pos], send_sem=z_send, recv_sem=z_recv,
             device_id=(me_t, (z_pos + step) % NZ * NW + w_pos), device_id_type=MESH,
@@ -180,6 +181,10 @@
             copy.start()
     partials[w_pos] = partial[w_pos]
     pltpu.make_async_copy(partials.at[pl.ds(0, NW - 1)], partials.at[pl.ds(0, NW - 1)], w_recv).wait()
+    for step in range(1, NX):
+        pl.semaphore_signal(
+            ready_sem, inc=1, device_id=((x_pos + step) % NX * NH + half, me_f), device_id_type=MESH
+        )
     sums = partials[0].astype(F32)
     for slot in range(1, NW):
         sums = sums + partials[slot].astype(F32)
@@ -233,15 +238,20 @@
             for slot, tile in enumerate(regroup(reals + imags)):
                 outgoing[column * 16 + slot] = tile.astype(BF16)
 
-    def send(step, carry):
-        target = (me_f + step) % NF
-        pltpu.make_async_remote_copy(
-            src_ref=outgoing.at[target], dst_ref=received.at[me_f], send_sem=f_send, recv_sem=f_recv,
-            device_id=(me_t, target), device_id_type=MESH,
-        ).start()
-        return carry
-
-    lax.fori_loop(1, NF, send, 0)
+    for target_z in (0, 1, 2, 3, 7, 4, 6, 5):
+        def send(step, carry, target_z=target_z):
+            target = target_z * NW + (w_pos + step) % NW
+
+            @pl.when(target != me_f)
+            def _():
+                pltpu.make_async_remote_copy(
+                    src_ref=outgoing.at[target], dst_ref=received.at[me_f], send_sem=f_send, recv_sem=f_recv,
+                    device_id=(me_t, target), device_id_type=MESH,
+                ).start()
+
+            return carry
+
+        lax.fori_loop(0, NW, send, 0)
     received[me_f] = outgoing[me_f]
     pltpu.make_async_copy(received.at[pl.ds(0, NF - 1)], received.at[pl.ds(0, NF - 1)], f_recv).wait()
 
@@ -260,29 +270,36 @@
             series[templ, 1, :, start : start + 256] = imag_part
             power = real_part * real_part + imag_part * imag_part
             top = power if top is None else jnp.maximum(top, power)
-        best[:, start : start + 256] = top
-
-    for step in range(1, NX):
+        bests[me_t, :, start : start + 256] = top.astype(BF16)
+
+    pl.semaphore_wait(ready_sem, NX - 1)
+    for away in ((2, 1), (1, 1), (3, 1), (0, 1), (2, 0), (1, 0), (3, 0)):
         pltpu.make_async_remote_copy(
-            src_ref=best, dst_ref=bests.at[x_pos], send_sem=x_send, recv_sem=x_recv,
-            device_id=((x_pos + step) % NX * NH + half, me_f), device_id_type=MESH,
+            src_ref=bests.at[me_t], dst_ref=bests.at[me_t], send_sem=t_send, recv_sem=t_recv,
+            device_id=((x_pos + away[0]) % NX * NH + (half + away[1]) % NH, me_f), device_id_type=MESH,
         ).start()
-    bests[x_pos] = best[...]
-    pltpu.make_async_copy(bests.at[pl.ds(0, NX - 1)], bests.at[pl.ds(0, NX - 1)], x_recv).wait()
-    top = jnp.maximum(jnp.maximum(bests[0], bests[1]), jnp.maximum(bests[2], bests[3]))
-    best_half[...] = top
-    last = pltpu.make_async_remote_copy(
-        src_ref=best_half, dst_ref=other_half, send_sem=h_send, recv_sem=h_recv,
-        device_id=(x_pos * NH + 1 - half, me_f), device_id_type=MESH,
-    )
-    last.start()
-    last.wait()
-    peak[...] = jnp.maximum(top, other_half[...])
+    others = NX * NH - 1
+    pltpu.make_async_copy(bests.at[pl.ds(0, others)], bests.at[pl.ds(0, others)], t_recv).wait()
+    tops = [bests[slot].astype(F32) for slot in range(NX * NH)]
+    while len(tops) > 1:
+        tops = [jnp.maximum(tops[i], tops[i + 1]) for i in range(0, len(tops), 2)]
+    peak[...] = tops[0]
 
     pltpu.make_async_copy(gathered.at[pl.ds(0, NZ - 1)], gathered.at[pl.ds(0, NZ - 1)], z_send).wait()
     pltpu.make_async_copy(partial.at[pl.ds(0, NW - 1)], partial.at[pl.ds(0, NW - 1)], w_send).wait()
     pltpu.make_async_copy(outgoing.at[pl.ds(0, NF - 1)], outgoing.at[pl.ds(0, NF - 1)], f_send).wait()
-    pltpu.make_async_copy(bests.at[pl.ds(0, NX - 1)], bests.at[pl.ds(0, NX - 1)], x_send).wait()
+    pltpu.make_async_copy(bests.at[pl.ds(0, others)], bests.at[pl.ds(0, others)], t_send).wait()
+
+
+def store(series_v, peak_v, series, peak, sems):
+    copies = [
+        pltpu.make_async_copy(series_v, series, sems.at[0]),
+        pltpu.make_async_copy(peak_v, peak, sems.at[1]),
+    ]
+    for copy in copies:
+        copy.start()
+    for copy in copies:
+        copy.wait()
 
 
 def local(strain, inv_asd, spectra, cutoff):
@@ -290,11 +307,11 @@
     anywhere = pl.BlockSpec(memory_space=pl.ANY)
     inside = pl.BlockSpec(memory_space=pltpu.VMEM)
     dma = pltpu.SemaphoreType.DMA
-    return pl.pallas_call(
+    series, peak = pl.pallas_call(
         kernel,
         out_shape=(
-            jax.ShapeDtypeStruct((TEMPL, 2, ROWS, SIDE), F32),
-            jax.ShapeDtypeStruct((ROWS, SIDE), F32),
+            pltpu.VMEM((TEMPL, 2, ROWS, SIDE), F32),
+            pltpu.VMEM((ROWS, SIDE), F32),
         ),
         in_specs=[anywhere] * 6,
         out_specs=(inside, inside),
@@ -311,14 +328,22 @@
             pltpu.VMEM((128, BAND), F32),
             pltpu.VMEM((NF, ROWS, 128), BF16),
             pltpu.VMEM((NF, ROWS, 128), BF16),
-            pltpu.VMEM((ROWS, SIDE), F32),
-            pltpu.VMEM((NX, ROWS, SIDE), F32),
-            pltpu.VMEM((ROWS, SIDE), F32),
-            pltpu.VMEM((ROWS, SIDE), F32),
-            dma((6,)), dma, dma, dma, dma, pltpu.SemaphoreType.REGULAR, dma, dma, dma, dma, dma, dma,
+            pltpu.VMEM((NX * NH, ROWS, SIDE), BF16),
+            dma((6,)), dma, dma, dma, dma, pltpu.SemaphoreType.REGULAR, pltpu.SemaphoreType.REGULAR,
+            dma, dma, dma, dma,
         ],
         compiler_params=pltpu.CompilerParams(collective_id=0, has_side_effects=True),
     )(strain, inv_asd, spectra, cutoff, jnp.asarray(high), jnp.asarray(low))
+    return pl.pallas_call(
+        store,
+        out_shape=(
+            jax.ShapeDtypeStruct((TEMPL, 2, ROWS, SIDE), F32),
+            jax.ShapeDtypeStruct((ROWS, SIDE), F32),
+        ),
+        in_specs=[anywhere, anywhere],
+        out_specs=(anywhere, anywhere),
+        scratch_shapes=[dma((2,))],
+    )(pltpu.with_memory_space_constraint(series, pltpu.VMEM), pltpu.with_memory_space_constraint(peak, pltpu.VMEM))
 
 
 def solution(mesh):

time: 43.2 us -> 37.8 us (0.87)
  Pallas kernels: 40.1 us -> 37 us
  local copies, waits for them, and re-layouts: 2.29 us -> 0 us
    pallas_call x1 -> x2, Pallas kernels: 40.1 us -> 37 us  [the longest x1 36.3 us: local(): pl.pallas_call(kernel, out_shape=(pltpu.VMEM((TEMPL, 2, ROWS, SIDE), F32)...]
    unnamed x4 -> x0, local copies, waits for them, and re-layouts: 2.29 us -> none
where the time goes in v2:
time: 37.8 us; the launch traced here: 37.6 us
  Pallas kernels  37 us (98%)
  between operations  0.64 us (2%)
    pallas_call x1, Pallas kernels, local(): pl.pallas_call(kernel, out_shape=(pltpu.VMEM((TEMPL, 2, ROWS, SIDE), F32)...  36.3 us

profile of v2, /device:TPU:1, one launch (start us, length us, event | category | flops | bytes accessed | tf_op | source)
XLA Modules:
  0.0 37.6 jit_solution(15474021147648232909)
XLA Ops:
  0.6 36.3 %shard_map.77 = (f32[8,2,8,512]{3,2,1,0:T(8,128)S(1)}, f32[8,512]{1,0:T(8,128)S(1)}) custom-call(f32[8,512]{1,0:T(8,128)} %strain.1, f32[8,512]{1,0:T(8,128)} %inv_asd.1, bf16[8,8,2,512]{3,2,1,0:T(2,128)(2,1)} %spectra.1, s32[8]{0:T(128)} %cutoff.1, bf16[512,1024]{1,0:T(8,128)(2,1)} %constant.4.clone.high_table, bf16[512,512]{1,0:T(8,128)(2,1)} %constant.5.clone.low_table), custom_call_target="tpu_custom_call" | custom-call | tf_op jit(solution)/shard_map/pallas_call | solution.py:310
  36.9 0.7 %shard_map.78 = (f32[8,2,8,512]{3,2,1,0:T(8,128)}, f32[8,512]{1,0:T(8,128)}) custom-call(f32[8,2,8,512]{3,2,1,0:T(8,128)S(1)} %get-tuple-element.4.series_v, f32[8,512]{1,0:T(8,128)S(1)} %get-tuple-element.5.peak_v), custom_call_target="tpu_custom_call" | custom-call | tf_op jit(solution)/shard_map/pallas_call | solution.py:337

commit v3 on v2

--- a/solution.py
+++ b/solution.py
@@ -22,7 +22,7 @@
 ROWS = SIDE // NF
 TEMPL = 8
 PAIRS = 2 * TEMPL
-FAR_FIRST = (4, 3, 5, 2, 6, 1, 7)
+EARLY = NZ // 2
 MESH = pl.DeviceIdType.MESH
 F32 = jnp.float32
 BF16 = jnp.bfloat16
@@ -73,8 +73,8 @@
 def kernel(
     strain, inv_asd, spectra, cutoff, high_table, low_table, series, peak,
     table, table_low, strain_v, asd_v, spectra_v, cut_s, gathered, partial, partials,
-    weights, outgoing, received, bests,
-    load_sem, z_send, z_recv, w_send, w_recv, done_sem, ready_sem, f_send, f_recv, t_send, t_recv,
+    weights, outgoing, received, bests, mirror_out, mirror_in, early_out, early_in, early_sum, mirror_sum,
+    load_sem, z_send, early_recv, late_recv, late_sem, o_send, o_recv, e_send, e_recv, m_send, m_recv, w_send, w_recv, done_sem, ready_sem, f_send, f_recv, t_send, t_recv,
 ):
     me_t = lax.axis_index("tmpl")
     me_f = lax.axis_index("freq")
@@ -101,8 +101,18 @@
     def greet(device):
         pl.semaphore_signal(barrier, inc=1, device_id=device, device_id_type=MESH)
 
-    for step in FAR_FIRST:
-        greet((me_t, (z_pos + step) % NZ * NW + w_pos))
+    early = z_pos < EARLY
+    late = jnp.logical_not(early)
+    mirror = NZ - 1 - z_pos
+    base_z = z_pos // EARLY * EARLY
+    for step in (3, 1, 2):
+        greet((me_t, (base_z + (z_pos + step) % EARLY) * NW + w_pos))
+
+    @pl.when(early)
+    def _():
+        for late_z in range(EARLY, NZ):
+            greet((me_t, late_z * NW + w_pos))
+
     for away in (3, 5, 2, 6, 1, 7):
         place = (y_full + away) % (NH * NY)
         for to_core in range(NC):
@@ -115,24 +125,87 @@
     own = strain_v[...]
     gathered[z_pos] = jnp.concatenate([own[:, :BAND], own[:, BAND:]], 0).astype(BF16)
 
-    pl.semaphore_wait(barrier, NZ - 1 + (NH * NY - 2) * NC + 1 + NX - 1)
-
-    for step in FAR_FIRST:
-        copy = pltpu.make_async_remote_copy(
-            src_ref=gathered.at[z_pos], dst_ref=gathered.at[z_pos], send_sem=z_send, recv_sem=z_recv,
-            device_id=(me_t, (z_pos + step) % NZ * NW + w_pos), device_id_type=MESH,
-        )
-        copy.start()
+    alike = EARLY - 1 + (NH * NY - 2) * NC + 1 + NX - 1
+
+    def give(to_z, recv_sem):
+        pltpu.make_async_remote_copy(
+            src_ref=gathered.at[z_pos], dst_ref=gathered.at[z_pos], send_sem=z_send, recv_sem=recv_sem,
+            device_id=(me_t, to_z * NW + w_pos), device_id_type=MESH,
+        ).start()
+
+    def arrived(count, sem):
+        pltpu.make_async_copy(gathered.at[pl.ds(0, count)], gathered.at[pl.ds(0, count)], sem).wait()
+
+    def tell_line():
+        for step in range(1, NW):
+            pl.semaphore_signal(
+                done_sem, inc=1, device_id=(me_t, z_pos * NW + (w_pos + step) % NW), device_id_type=MESH
+            )
+
+    def first_table(z_rows, z_first):
+        row = iota((128, 64), 0)
+        col = iota((128, 64), 1)
+        freq_row = 64 * z_rows + 8 * (row // 16) + row % 8
+        sample_row = 64 * (z_first + col // 16) + 8 * w_pos + col % 8
+        turns = (freq_row * sample_row + 128 * (row // 8 % 2)) & (SIDE - 1)
+        values = jnp.cos(turns.astype(F32) * (2.0 * math.pi / SIDE))
+        side = col // 8 % 2
+        return jnp.concatenate([jnp.where(side == 0, values, 0.0), jnp.where(side == 1, values, 0.0)], 0)
+
+    def to_group(source, target, send_sem, recv_sem):
+        for step, to_core in ((2, 0), (2, 1), (1, 0), (1, 1), (3, 0), (3, 1), (0, 1)):
+            if step == 2:
+                place = (y_full + (2 if to_core == 0 else 6)) % (NH * NY)
+            else:
+                place = (y_full + (0, 1, 0, 7)[step]) % (NH * NY)
+            target_w = place % NY * NC + (1 - core if step == 0 else to_core)
+            pltpu.make_async_remote_copy(
+                src_ref=source.at[target_w], dst_ref=target.at[w_pos], send_sem=send_sem, recv_sem=recv_sem,
+                device_id=(x_pos * NH + place // NY, z_pos * NW + target_w), device_id_type=MESH,
+            ).start()
+        target[w_pos] = source[w_pos]
+
+    def first_share(tables, first_z, out):
+        blocks = gathered[first_z : first_z + EARLY].reshape(64, BAND)
+        shares = dot(tables[0], blocks) + dot(tables[1], blocks)
+        out[:, :, :BAND] = shares[:128].reshape(NW, 16, BAND).astype(BF16)
+        out[:, :, BAND:] = shares[128:].reshape(NW, 16, BAND).astype(BF16)
+
+    def total(ref):
+        sums = ref[0].astype(F32)
+        for slot in range(1, NW):
+            sums = sums + ref[slot].astype(F32)
+        return sums
+
+    def came(ref, sem):
+        pltpu.make_async_copy(ref.at[pl.ds(0, NW - 1)], ref.at[pl.ds(0, NW - 1)], sem).wait()
+
+    @pl.when(late)
+    def _():
+        pl.semaphore_wait(barrier, alike + EARLY)
+        for step in (3, 1, 2):
+            give(EARLY + (z_pos + step) % EARLY, late_recv)
+        for to_z in range(EARLY):
+            give(to_z, late_recv)
+        pl.semaphore_signal(late_sem, inc=1, device_id=(me_t, mirror * NW + w_pos), device_id_type=MESH)
+        tell_line()
+
+    @pl.when(early)
+    def _():
+        pl.semaphore_wait(barrier, alike)
+        for step in (3, 1, 2):
+            give((z_pos + step) % EARLY, early_recv)
+        mirror_tables = split(first_table(mirror, 0))
+        own_tables = split(first_table(z_pos, 0))
+        arrived(EARLY - 1, early_recv)
+        first_share(mirror_tables, 0, mirror_out)
+        to_group(mirror_out, mirror_in, o_send, o_recv)
+        first_share(own_tables, 0, early_out)
+        to_group(early_out, early_in, e_send, e_recv)
 
     row = iota((128, 128), 0)
     col = iota((128, 128), 1)
-    freq_row = 64 * z_pos + 8 * (row // 16) + row % 8
-    sample_row = 64 * (col // 16) + 8 * w_pos + col % 8
-    turns = (freq_row * sample_row + 128 * (row // 8 % 2)) & (SIDE - 1)
-    first = jnp.cos(turns.astype(F32) * (2.0 * math.pi / SIDE))
-    side = col // 8 % 2
-    first = jnp.concatenate([jnp.where(side == 0, first, 0.0), jnp.where(side == 1, first, 0.0)], 0)
-    first_high, first_low = split(first)
+    late_tables = split(first_table(z_pos, EARLY))
     twist = (ROWS * me_f + iota((ROWS, SIDE), 0)) * iota((ROWS, SIDE), 1)
     twist = twist.astype(F32) * (2.0 * math.pi / TOTAL)
     twist_cos = jnp.cos(twist)
@@ -152,42 +225,40 @@
             block = slice((part * TEMPL + templ) * ROWS, (part * TEMPL + templ + 1) * ROWS)
             weights[block, :] = sorted_spectra[block, :] * gain
 
-    pltpu.make_async_copy(gathered.at[pl.ds(0, NZ - 1)], gathered.at[pl.ds(0, NZ - 1)], z_recv).wait()
-    for step in range(1, NW):
-        pl.semaphore_signal(
-            done_sem, inc=1, device_id=(me_t, z_pos * NW + (w_pos + step) % NW), device_id_type=MESH
-        )
-    blocks = gathered[...].reshape(128, BAND)
-    shares = dot(first_high, blocks) + dot(first_low, blocks)
-    partial[:, :, :BAND] = shares[:128].reshape(NW, 16, BAND).astype(BF16)
-    partial[:, :, BAND:] = shares[128:].reshape(NW, 16, BAND).astype(BF16)
-    for step in range(NY):
-        for to_core in range(NC):
-            if step == 2:
-                away = 2 if to_core == 0 else 6
-            else:
-                away = (0, 1, 2, 7)[step]
-            place = (y_full + away) % (NH * NY)
-            target_core = to_core
-            target_w = place % NY * NC + target_core
-            if step == 0:
-                if to_core == 0:
-                    continue
-                target_w = w_pos // NC * NC + (1 - core)
-            copy = pltpu.make_async_remote_copy(
-                src_ref=partial.at[target_w], dst_ref=partials.at[w_pos], send_sem=w_send, recv_sem=w_recv,
-                device_id=(x_pos * NH + place // NY, z_pos * NW + target_w), device_id_type=MESH,
-            )
-            copy.start()
-    partials[w_pos] = partial[w_pos]
-    pltpu.make_async_copy(partials.at[pl.ds(0, NW - 1)], partials.at[pl.ds(0, NW - 1)], w_recv).wait()
+    @pl.when(early)
+    def _():
+        came(mirror_in, o_recv)
+        mirror_sum[...] = total(mirror_in)
+        pl.semaphore_wait(late_sem, 1)
+        pltpu.make_async_remote_copy(
+            src_ref=mirror_sum, dst_ref=early_sum, send_sem=m_send, recv_sem=m_recv,
+            device_id=(me_t, mirror * NW + w_pos), device_id_type=MESH,
+        ).start()
+        arrived(EARLY, late_recv)
+
+    @pl.when(late)
+    def _():
+        arrived(EARLY - 1, late_recv)
+
+    first_share(late_tables, EARLY, partial)
+    to_group(partial, partials, w_send, w_recv)
+
+    @pl.when(early)
+    def _():
+        tell_line()
+        came(early_in, e_recv)
+        early_sum[...] = total(early_in)
+
+    @pl.when(late)
+    def _():
+        pltpu.make_async_copy(mirror_sum, early_sum, m_recv).wait()
+
+    came(partials, w_recv)
     for step in range(1, NX):
         pl.semaphore_signal(
             ready_sem, inc=1, device_id=((x_pos + step) % NX * NH + half, me_f), device_id_type=MESH
         )
-    sums = partials[0].astype(F32)
-    for slot in range(1, NW):
-        sums = sums + partials[slot].astype(F32)
+    sums = early_sum[...] + total(partials)
     sum_real = sums[:ROWS]
     sum_imag = sums[ROWS:]
     turned = jnp.concatenate(
@@ -285,8 +356,18 @@
         tops = [jnp.maximum(tops[i], tops[i + 1]) for i in range(0, len(tops), 2)]
     peak[...] = tops[0]
 
-    pltpu.make_async_copy(gathered.at[pl.ds(0, NZ - 1)], gathered.at[pl.ds(0, NZ - 1)], z_send).wait()
-    pltpu.make_async_copy(partial.at[pl.ds(0, NW - 1)], partial.at[pl.ds(0, NW - 1)], w_send).wait()
+    @pl.when(early)
+    def _():
+        arrived(EARLY - 1, z_send)
+        came(mirror_out, o_send)
+        came(early_out, e_send)
+        pltpu.make_async_copy(mirror_sum, early_sum, m_send).wait()
+
+    @pl.when(late)
+    def _():
+        arrived(NZ - 1, z_send)
+
+    came(partial, w_send)
     pltpu.make_async_copy(outgoing.at[pl.ds(0, NF - 1)], outgoing.at[pl.ds(0, NF - 1)], f_send).wait()
     pltpu.make_async_copy(bests.at[pl.ds(0, others)], bests.at[pl.ds(0, others)], t_send).wait()
 
@@ -329,7 +410,14 @@
             pltpu.VMEM((NF, ROWS, 128), BF16),
             pltpu.VMEM((NF, ROWS, 128), BF16),
             pltpu.VMEM((NX * NH, ROWS, SIDE), BF16),
-            dma((6,)), dma, dma, dma, dma, pltpu.SemaphoreType.REGULAR, pltpu.SemaphoreType.REGULAR,
+            pltpu.VMEM((NW, 16, SIDE), BF16),
+            pltpu.VMEM((NW, 16, SIDE), BF16),
+            pltpu.VMEM((NW, 16, SIDE), BF16),
+            pltpu.VMEM((NW, 16, SIDE), BF16),
+            pltpu.VMEM((16, SIDE), F32),
+            pltpu.VMEM((16, SIDE), F32),
+            dma((6,)), dma, dma, dma, pltpu.SemaphoreType.REGULAR, dma, dma, dma, dma, dma, dma, dma, dma,
+            pltpu.SemaphoreType.REGULAR, pltpu.SemaphoreType.REGULAR,
             dma, dma, dma, dma,
         ],
         compiler_params=pltpu.CompilerParams(collective_id=0, has_side_effects=True),

time: 37.8 us -> 37.3 us (0.987)
  Pallas kernels: 37 us -> 36.5 us
    pallas_call x1, Pallas kernels: 36.3 us -> 35.8 us  [local(): pl.pallas_call(kernel, out_shape=(pltpu.VMEM((TEMPL, 2, ROWS, SIDE), F32)...]
where the time goes in v3:
time: 37.3 us; the launch traced here: 37.2 us
  Pallas kernels  36.5 us (98%)
  between operations  0.64 us (2%)
    pallas_call x1, Pallas kernels, local(): pl.pallas_call(kernel, out_shape=(pltpu.VMEM((TEMPL, 2, ROWS, SIDE), F32)...  35.8 us

profile of v3, /device:TPU:1, one launch (start us, length us, event | category | flops | bytes accessed | tf_op | source)
XLA Modules:
  0.0 37.2 jit_solution(4370152439295358773)
XLA Ops:
  0.6 35.8 %shard_map.77 = (f32[8,2,8,512]{3,2,1,0:T(8,128)S(1)}, f32[8,512]{1,0:T(8,128)S(1)}) custom-call(f32[8,512]{1,0:T(8,128)} %strain.1, f32[8,512]{1,0:T(8,128)} %inv_asd.1, bf16[8,8,2,512]{3,2,1,0:T(2,128)(2,1)} %spectra.1, s32[8]{0:T(128)} %cutoff.1, bf16[512,1024]{1,0:T(8,128)(2,1)} %constant.4.clone.high_table, bf16[512,512]{1,0:T(8,128)(2,1)} %constant.5.clone.low_table), custom_call_target="tpu_custom_call" | custom-call | tf_op jit(solution)/shard_map/pallas_call | solution.py:391
  36.4 0.7 %shard_map.78 = (f32[8,2,8,512]{3,2,1,0:T(8,128)}, f32[8,512]{1,0:T(8,128)}) custom-call(f32[8,2,8,512]{3,2,1,0:T(8,128)S(1)} %get-tuple-element.4.series_v, f32[8,512]{1,0:T(8,128)S(1)} %get-tuple-element.5.peak_v), custom_call_target="tpu_custom_call" | custom-call | tf_op jit(solution)/shard_map/pallas_call | solution.py:425

commit v4 on v3

--- a/solution.py
+++ b/solution.py
@@ -287,42 +287,40 @@
         product.append(spec_imag * gain_real - spec_real * gain_imag)
     product = jnp.concatenate(product, 0).astype(BF16)
 
-    pl.semaphore_wait(done_sem, NW - 1)
-    for pair in range(2):
-        start = pair * 256
-        by_cos = dot(product, table[:BAND, start : start + 256])
-        by_sin = dot(product, table[:BAND, SIDE + start : SIDE + start + 256])
-        for inner in range(2):
-            column = 2 * pair + inner
-            here = slice(inner * 128, (inner + 1) * 128)
-            cos_here = twist_cos[:, column * 128 : (column + 1) * 128]
-            sin_here = twist_sin[:, column * 128 : (column + 1) * 128]
-            reals = []
-            imags = []
-            for templ in range(TEMPL):
-                up = slice(templ * ROWS, (templ + 1) * ROWS)
-                down = slice((TEMPL + templ) * ROWS, (TEMPL + templ + 1) * ROWS)
-                real_part = by_cos[up, here] - by_sin[down, here]
-                imag_part = by_sin[up, here] + by_cos[down, here]
-                reals.append(real_part * cos_here - imag_part * sin_here)
-                imags.append(real_part * sin_here + imag_part * cos_here)
-            for slot, tile in enumerate(regroup(reals + imags)):
-                outgoing[column * 16 + slot] = tile.astype(BF16)
-
-    for target_z in (0, 1, 2, 3, 7, 4, 6, 5):
-        def send(step, carry, target_z=target_z):
-            target = target_z * NW + (w_pos + step) % NW
-
-            @pl.when(target != me_f)
-            def _():
-                pltpu.make_async_remote_copy(
-                    src_ref=outgoing.at[target], dst_ref=received.at[me_f], send_sem=f_send, recv_sem=f_recv,
-                    device_id=(me_t, target), device_id_type=MESH,
-                ).start()
-
-            return carry
-
-        lax.fori_loop(0, NW, send, 0)
+    def send(target):
+        pltpu.make_async_remote_copy(
+            src_ref=outgoing.at[target], dst_ref=received.at[me_f], send_sem=f_send, recv_sem=f_recv,
+            device_id=(me_t, target), device_id_type=MESH,
+        ).start()
+
+    for column, target_zs in ((0, (0, 1)), (1, (2, 3)), (3, (7, 6)), (2, (4, 5))):
+        start = column * 128
+        by_cos = dot(product, table[:BAND, start : start + 128])
+        by_sin = dot(product, table[:BAND, SIDE + start : SIDE + start + 128])
+        cos_here = twist_cos[:, start : start + 128]
+        sin_here = twist_sin[:, start : start + 128]
+        reals = []
+        imags = []
+        for templ in range(TEMPL):
+            up = slice(templ * ROWS, (templ + 1) * ROWS)
+            down = slice((TEMPL + templ) * ROWS, (TEMPL + templ + 1) * ROWS)
+            real_part = by_cos[up] - by_sin[down]
+            imag_part = by_sin[up] + by_cos[down]
+            reals.append(real_part * cos_here - imag_part * sin_here)
+            imags.append(real_part * sin_here + imag_part * cos_here)
+        for slot, tile in enumerate(regroup(reals + imags)):
+            outgoing[column * 16 + slot] = tile.astype(BF16)
+        if column == 0:
+            pl.semaphore_wait(done_sem, NW - 1)
+        for target_z in target_zs:
+
+            def send_row(step, carry, target_z=target_z):
+                target = target_z * NW + (w_pos + step) % NW
+                pl.when(target != me_f)(functools.partial(send, target))
+                return carry
+
+            lax.fori_loop(0, NW, send_row, 0)
+
     received[me_f] = outgoing[me_f]
     pltpu.make_async_copy(received.at[pl.ds(0, NF - 1)], received.at[pl.ds(0, NF - 1)], f_recv).wait()
 

time: 37.3 us -> 37.1 us (level)
  no operation moved by 1% of the time
where the time goes in v4:
time: 37.1 us; the launch traced here: 37 us
  Pallas kernels  36.3 us (98%)
  between operations  0.64 us (2%)
    pallas_call x1, Pallas kernels, local(): pl.pallas_call(kernel, out_shape=(pltpu.VMEM((TEMPL, 2, ROWS, SIDE), F32)...  35.6 us

profile of v4, /device:TPU:1, one launch (start us, length us, event | category | flops | bytes accessed | tf_op | source)
XLA Modules:
  0.0 37.0 jit_solution(13056144002467171959)
XLA Ops:
  0.6 35.6 %shard_map.77 = (f32[8,2,8,512]{3,2,1,0:T(8,128)S(1)}, f32[8,512]{1,0:T(8,128)S(1)}) custom-call(f32[8,512]{1,0:T(8,128)} %strain.1, f32[8,512]{1,0:T(8,128)} %inv_asd.1, bf16[8,8,2,512]{3,2,1,0:T(2,128)(2,1)} %spectra.1, s32[8]{0:T(128)} %cutoff.1, bf16[512,1024]{1,0:T(8,128)(2,1)} %constant.4.clone.high_table, bf16[512,512]{1,0:T(8,128)(2,1)} %constant.5.clone.low_table), custom_call_target="tpu_custom_call" | custom-call | tf_op jit(solution)/shard_map/pallas_call | solution.py:389
  36.2 0.7 %shard_map.78 = (f32[8,2,8,512]{3,2,1,0:T(8,128)}, f32[8,512]{1,0:T(8,128)}) custom-call(f32[8,2,8,512]{3,2,1,0:T(8,128)S(1)} %get-tuple-element.4.series_v, f32[8,512]{1,0:T(8,128)S(1)} %get-tuple-element.5.peak_v), custom_call_target="tpu_custom_call" | custom-call | tf_op jit(solution)/shard_map/pallas_call | solution.py:423

commit v5 on v4

--- a/solution.py
+++ b/solution.py
@@ -105,6 +105,10 @@
     late = jnp.logical_not(early)
     mirror = NZ - 1 - z_pos
     base_z = z_pos // EARLY * EARLY
+    for away in (3, 5):
+        place = (y_full + away) % (NH * NY)
+        for to_core in range(NC):
+            greet((x_pos * NH + place // NY, z_pos * NW + place % NY * NC + to_core))
     for step in (3, 1, 2):
         greet((me_t, (base_z + (z_pos + step) % EARLY) * NW + w_pos))
 
@@ -113,7 +117,7 @@
         for late_z in range(EARLY, NZ):
             greet((me_t, late_z * NW + w_pos))
 
-    for away in (3, 5, 2, 6, 1, 7):
+    for away in (2, 6, 1, 7):
         place = (y_full + away) % (NH * NY)
         for to_core in range(NC):
             greet((x_pos * NH + place // NY, z_pos * NW + place % NY * NC + to_core))

time: 37.1 us -> 37.1 us (level)
  no operation moved by 1% of the time
where the time goes in v5:
time: 37.1 us; the launch traced here: 36.9 us
  Pallas kernels  36.3 us (98%)
  between operations  0.64 us (2%)
    pallas_call x1, Pallas kernels, local(): pl.pallas_call(kernel, out_shape=(pltpu.VMEM((TEMPL, 2, ROWS, SIDE), F32)...  35.6 us

profile of v5, /device:TPU:1, one launch (start us, length us, event | category | flops | bytes accessed | tf_op | source)
XLA Modules:
  0.0 36.9 jit_solution(16262059850634676175)
XLA Ops:
  0.6 35.6 %shard_map.77 = (f32[8,2,8,512]{3,2,1,0:T(8,128)S(1)}, f32[8,512]{1,0:T(8,128)S(1)}) custom-call(f32[8,512]{1,0:T(8,128)} %strain.1, f32[8,512]{1,0:T(8,128)} %inv_asd.1, bf16[8,8,2,512]{3,2,1,0:T(2,128)(2,1)} %spectra.1, s32[8]{0:T(128)} %cutoff.1, bf16[512,1024]{1,0:T(8,128)(2,1)} %constant.4.clone.high_table, bf16[512,512]{1,0:T(8,128)(2,1)} %constant.5.clone.low_table), custom_call_target="tpu_custom_call" | custom-call | tf_op jit(solution)/shard_map/pallas_call | solution.py:393
  36.2 0.7 %shard_map.78 = (f32[8,2,8,512]{3,2,1,0:T(8,128)}, f32[8,512]{1,0:T(8,128)}) custom-call(f32[8,2,8,512]{3,2,1,0:T(8,128)S(1)} %get-tuple-element.4.series_v, f32[8,512]{1,0:T(8,128)S(1)} %get-tuple-element.5.peak_v), custom_call_target="tpu_custom_call" | custom-call | tf_op jit(solution)/shard_map/pallas_call | solution.py:427
